TPU v7x, 256 devices: a whole 4x4x8 slice. The times are simulated.
256 devices in a mesh: leaf: 16 (over y_lo, x, core), samp: 16 (over z, y_hi).
Axes of the slice: x: 4, y: 4 (y_hi: 2, y_lo: 2; y = y_hi * 2 + y_lo), z: 8, core: 2. Of those that a mesh axis runs over, the one named last changes fastest.
Arguments:
- limits: float32 [8, 16, 512], P(None, 'leaf'), may hold values from -1.25 to 2.25
- inv_scale: float32 [8, 16, 512], P(None, 'leaf'), may hold values from 0.5 to 1.5
- lower_blocks: bfloat16 [8, 16, 512, 512], P(None, 'leaf'), may hold values from -0.19921875 to 0.19921875
- qmc_gen: int32 [8, 16, 512], P(None, 'leaf'), may hold values from 1 to 8191
- col_one: bfloat16 [8, 16, 512, 64], P(None, 'leaf'), may hold values from -0.75 to 0.75
- row_one: bfloat16 [8, 16, 512, 64], P(None, 'leaf'), may hold values from -0.25 to 0.25
- col_two: bfloat16 [8, 16, 512, 64], P(None, 'leaf'), may hold values from -0.75 to 0.75
- row_two: bfloat16 [8, 16, 512, 64], P(None, 'leaf'), may hold values from -0.25 to 0.25
Outputs:
- draws: bfloat16 [8, 16, 512, 8192], P(None, 'leaf', None, 'samp')
- mean_log: float32 [8, 16], P(None, 'leaf')
- sample_log: float32 [8192], P('samp')
Inputs may be any that keep to these rules, and one draw needn't show every extreme that they name: `qmc_gen`: A rank-one lattice rule's generating vector.
All inputs are finite; a program needn't handle non-finite values.
Results may differ from a plain program's by a relative error of at most 0.006.
Values may be sent and summed in bfloat16 or wider, within the bound.
A program may use at most 64 MiB of HBM per device.

v0:
```python
import jax
import jax.numpy as jnp
from jax import lax
from jax.sharding import PartitionSpec as P

M = 512
SUB = 128
SAMP_DEV = 512


coef_a = (
    -39.69683028665376,
    220.9460984245205,
    -275.9285104469687,
    138.357751867269,
    -30.66479806614716,
    2.506628277459239,
)
coef_b = (
    -54.47609879822406,
    161.5858368580409,
    -155.6989798598866,
    66.80131188771972,
    -13.28068155288572,
)
coef_c = (
    -0.007784894002430293,
    -0.3223964580411365,
    -2.400758277161838,
    -2.549732539343734,
    4.374664141464968,
    2.938163982698783,
)
coef_d = (0.007784695709041462, 0.3224671290700398, 2.445134137142996, 3.754408661907416)
inv_root_two = 0.7071067811865476
split_low = 0.02425


def partner(array, axis, distance):
    return lax.ppermute(array, axis, [(i, i ^ 1 << distance) for i in range(lax.axis_size(axis))])


def normal_cdf(value):
    return 0.5 * lax.erfc(-value * inv_root_two)


def log_normal_cdf(value):
    return jnp.log(normal_cdf(value))


def horner(coefs, value):
    total = coefs[0] + 0.0 * value
    for entry in coefs[1:]:
        total = total * value + entry
    return total


def tail_value(prob):
    safe = jnp.clip(prob, 1e-30, split_low)
    qvalue = jnp.sqrt(-2.0 * jnp.log(safe))
    return horner(coef_c, qvalue) / (horner(coef_d, qvalue) * qvalue + 1.0)


def normal_quantile(prob):
    centre = jnp.clip(prob, split_low, 1.0 - split_low) - 0.5
    square = centre * centre
    middle = horner(coef_a, square) * centre / (horner(coef_b, square) * square + 1.0)
    lower = tail_value(prob)
    upper = -tail_value(1.0 - prob)
    return jnp.where(prob < split_low, lower, jnp.where(prob > 1.0 - split_low, upper, middle))


def leaf_pass(lower_loc, scale_loc, limit_loc, points, shift_all):
    pieces = []
    logsum = jnp.zeros((points.shape[0], points.shape[2]), jnp.float32)
    for block in range(M // SUB):
        row_begin = block * SUB
        row_end = row_begin + SUB
        centred = jnp.broadcast_to(
            limit_loc[:, row_begin:row_end, None], (points.shape[0], SUB, points.shape[2])
        )
        if shift_all is not None:
            centred = centred - shift_all[:, row_begin:row_end]
        if block > 0:
            earlier = jnp.concatenate(pieces, axis=1)
            centred = centred - jnp.einsum(
                "ipq,iqn->ipn",
                lower_loc[:, row_begin:row_end, :row_begin],
                earlier,
                preferred_element_type=jnp.float32,
            )
        scaled = jnp.maximum(scale_loc[:, row_begin:row_end, None] * centred, -6.0)
        sample_block = normal_quantile(points[:, row_begin:row_end] * normal_cdf(scaled)).astype(
            jnp.bfloat16
        )
        logsum = logsum + jnp.sum(log_normal_cdf(scaled), axis=1)
        pieces.append(sample_block)
    return (jnp.concatenate(pieces, axis=1), logsum)


def contract(row_basis, samples):
    return jnp.einsum("iqr,iqn->irn", row_basis, samples, preferred_element_type=jnp.float32)


def expand(col_basis, coefs):
    return jnp.einsum("imr,irn->imn", col_basis, coefs, preferred_element_type=jnp.float32)


def per_device(limits, inv_scale, lower_blocks, qmc_gen, col_one, row_one, col_two, row_two):
    limit_loc = limits[:, 0]
    scale_loc = inv_scale[:, 0]
    lower_loc = lower_blocks[:, 0]
    gen_loc = qmc_gen[:, 0]
    col_first = col_one[:, 0]
    row_first = row_one[:, 0]
    col_second = col_two[:, 0]
    row_second = row_two[:, 0]
    sample_total = SAMP_DEV * lax.axis_size("samp")
    sample_index = lax.axis_index("samp") * SAMP_DEV + lax.iota(jnp.int32, SAMP_DEV)
    residue = sample_index[None, None, :] * gen_loc[:, :, None] % sample_total
    points = (residue.astype(jnp.float32) + 0.5) / sample_total
    draws_a, unused = leaf_pass(lower_loc, scale_loc, limit_loc, points, None)
    coef_sibling = partner(contract(row_first, draws_a).astype(jnp.bfloat16), "leaf", 0)
    shift_one = expand(col_first, coef_sibling)
    draws_b, unused = leaf_pass(lower_loc, scale_loc, limit_loc, points, shift_one)
    partial_value = contract(row_second, draws_b)
    pair_sum = (partial_value + partner(partial_value, "leaf", 0)).astype(jnp.bfloat16)
    group_sum = partner(pair_sum, "leaf", 1)
    shift_two = shift_one + expand(col_second, group_sum)
    draws_c, logsum = leaf_pass(lower_loc, scale_loc, limit_loc, points, shift_two)
    local_peak = jnp.max(logsum, axis=1)
    peak = lax.pmax(local_peak, "samp")
    mass = lax.psum(jnp.sum(jnp.exp(logsum - peak[:, None]), axis=1), "samp")
    sample_sums = jnp.sum(logsum, axis=0)
    sample_total_log = lax.psum(sample_sums, "leaf")
    mean_log = ((peak + jnp.log(mass / sample_total)) / M)[:, None]
    sample_log = sample_total_log / (draws_c.shape[0] * lax.axis_size("leaf") * M)
    return (draws_c[:, None], mean_log, sample_log)


def solution(mesh):
    return jax.shard_map(
        per_device,
        mesh=mesh,
        in_specs=(
            P(None, "leaf", None),
            P(None, "leaf", None),
            P(None, "leaf", None, None),
            P(None, "leaf", None),
            P(None, "leaf", None, None),
            P(None, "leaf", None, None),
            P(None, "leaf", None, None),
            P(None, "leaf", None, None),
        ),
        out_specs=(P(None, "leaf", None, "samp"), P(None, "leaf"), P("samp")),
        check_vma=False,
    )
```

profile of v0, /device:TPU:2, one launch (start us, length us, event | category | flops | bytes accessed | tf_op | source)
XLA Modules:
  0.0 296.7 jit_solution(15656126834247968204)
XLA Ops:
  0.6 0.0 copy-start
  0.6 0.8 copy_bitcast_fusion
  1.5 0.7 copy.19
  2.2 0.0 copy-start.3
  2.2 4.2 %fusion.2 = f32[8,512,512]{2,1,0:T(8,128)S(1)} fusion(s32[8,512]{1,0:T(8,128)S(1)} %bitcast.246, s32[512]{0:T(512)S(1)} %iota_add_fusion), kind=kLoop, calls=%fused_computation.7 | loop fusion | flops 31457280 | bytes 8407040 | tf_op jit(solution)/shard_map/div | solution.py:121
  6.5 8.3 %select_convert_fusion.11 = bf16[8,128,512]{2,1,0:T(8,128)(2,1)S(1)} fusion(f32[8,512,512]{2,1,0:T(8,128)S(1)} %fusion.2, f32[8,128]{1,0:T(8,128)S(1)} %get-tuple-element.36, f32[8,128]{1,0:T(8,128)S(1)} %get-tuple-element.37, f32[8,128]{1,0:T(8,128)S(1)} %get-tuple-element.35, f32[8,128]{1,0:T(8,128)S(1)} %get-tuple-element.34, ...), kind=kLoop, calls=%fused_computation.423 | loop fusion | flops 47710208 | bytes 3166208 | tf_op jit(solution)/shard_map/convert_element_type | solution.py:93
  14.8 0.0 copy-done.3
  14.8 13.1 %select_convert_fusion.10 = bf16[8,128,512]{2,1,0:T(8,128)(2,1)S(1)} fusion(f32[8,512,512]{2,1,0:T(8,128)S(1)} %fusion.2, bf16[8,128,512]{2,1,0:T(8,128)(2,1)S(1)} %select_convert_fusion.11, f32[8,128]{1,0:T(8,128)S(1)} %get-tuple-element.30, f32[8,128]{1,0:T(8,128)S(1)} %get-tuple-element.26, bf16[8,512,512]{2,1,0:T(8,128)(2,1)S(1)} %bitcast.247), kind=kOutput, calls=%fused_computation.399 | convolution fusion | flops 212860928 | bytes 4464640 | tf_op jit(solution)/shard_map/ipq,iqn->ipn/dot_general | solution.py:86
  27.9 13.2 %select_convert_fusion.9 = bf16[8,128,512]{2,1,0:T(8,128)(2,1)S(1)} fusion(f32[8,512,512]{2,1,0:T(8,128)S(1)} %fusion.2, bf16[8,128,512]{2,1,0:T(8,128)(2,1)S(1)} %select_convert_fusion.10, bf16[8,128,512]{2,1,0:T(8,128)(2,1)S(1)} %select_convert_fusion.11, f32[8,128]{1,0:T(8,128)S(1)} %get-tuple-element.29, f32[8,128]{1,0:T(8,128)S(1)} %get-tuple-element.25, ...), kind=kOutput, calls=%fused_computation.375 | convolution fusion | flops 351272960 | bytes 5775360 | tf_op jit(solution)/shard_map/ipq,iqn->ipn/dot_general | solution.py:86
  41.1 0.0 copy-start.4
  41.1 13.6 %select_convert_fusion.8 = bf16[8,128,512]{2,1,0:T(8,128)(2,1)S(1)} fusion(f32[8,512,512]{2,1,0:T(8,128)S(1)} %fusion.2, bf16[8,128,512]{2,1,0:T(8,128)(2,1)S(1)} %select_convert_fusion.9, bf16[8,128,512]{2,1,0:T(8,128)(2,1)S(1)} %select_convert_fusion.10, bf16[8,128,512]{2,1,0:T(8,128)(2,1)S(1)} %select_convert_fusion.11, ...), kind=kOutput, calls=%fused_computation.351 | convolution fusion | flops 490733568 | bytes 7086080 | tf_op jit(solution)/shard_map/ipq,iqn->ipn/dot_general | solution.py:86
  54.7 0.0 copy-done.4
  54.7 1.0 fusion.288
  55.7 0.3 collective-permute-start
  55.9 1.9 collective-permute-done
  57.8 0.0 copy-done
  57.8 1.3 convolution_bitcast_fusion
  59.1 12.8 %select_convert_fusion.7 = bf16[8,128,512]{2,1,0:T(8,128)(2,1)S(1)} fusion(f32[8,512,512]{2,1,0:T(8,128)S(1)} %convolution_bitcast_fusion, f32[8,512,512]{2,1,0:T(8,128)S(1)} %fusion.2, f32[8,128]{1,0:T(8,128)S(1)} %get-tuple-element.27, f32[8,128]{1,0:T(8,128)S(1)} %get-tuple-element.23), kind=kLoop, calls=%fused_computation.328 | loop fusion | flops 78643200 | bytes 5251072 | tf_op jit(solution)/shard_map/convert_element_type | solution.py:93
  71.9 13.2 %select_convert_fusion.6 = bf16[8,128,512]{2,1,0:T(8,128)(2,1)S(1)} fusion(f32[8,512,512]{2,1,0:T(8,128)S(1)} %convolution_bitcast_fusion, f32[8,512,512]{2,1,0:T(8,128)S(1)} %fusion.2, bf16[8,128,512]{2,1,0:T(8,128)(2,1)S(1)} %select_convert_fusion.7, f32[8,128]{1,0:T(8,128)S(1)} %get-tuple-element.30, f32[8,128]{1,0:T(8,128)S(1)} %get-tuple-element.26, ...), kind=kOutput, calls=%fused_computation.305 | convolution fusion | flops 213385216 | bytes 6561792 | tf_op jit(solution)/shard_map/ipq,iqn->ipn/dot_general | solution.py:86
  85.1 13.3 %select_convert_fusion.5 = bf16[8,128,512]{2,1,0:T(8,128)(2,1)S(1)} fusion(f32[8,512,512]{2,1,0:T(8,128)S(1)} %convolution_bitcast_fusion, f32[8,512,512]{2,1,0:T(8,128)S(1)} %fusion.2, bf16[8,128,512]{2,1,0:T(8,128)(2,1)S(1)} %select_convert_fusion.6, bf16[8,128,512]{2,1,0:T(8,128)(2,1)S(1)} %select_convert_fusion.7, f32[8,128]{1,0:T(8,128)S(1)} %get-tuple-element.29, ...), kind=kOutput, calls=%fused_computation.282 | convolution fusion | flops 351797248 | bytes 7872512 | tf_op jit(solution)/shard_map/ipq,iqn->ipn/dot_general | solution.py:86
  98.4 0.0 copy-start.5
  98.4 13.7 %select_convert_fusion.4 = bf16[8,128,512]{2,1,0:T(8,128)(2,1)S(1)} fusion(f32[8,512,512]{2,1,0:T(8,128)S(1)} %convolution_bitcast_fusion, f32[8,512,512]{2,1,0:T(8,128)S(1)} %fusion.2, bf16[8,128,512]{2,1,0:T(8,128)(2,1)S(1)} %select_convert_fusion.5, bf16[8,128,512]{2,1,0:T(8,128)(2,1)S(1)} %select_convert_fusion.6, ...), kind=kOutput, calls=%fused_computation.259 | convolution fusion | flops 491257856 | bytes 9183232 | tf_op jit(solution)/shard_map/ipq,iqn->ipn/dot_general | solution.py:86
  112.1 0.0 copy-done.5
  112.1 1.2 fusion.282
  113.4 0.0 copy-start.2
  113.4 0.2 collective-permute-start.1
  113.6 2.5 collective-permute-done.1
  116.1 0.3 add_convert_fusion
  116.4 2.5 collective-permute-start.2
  118.9 12.2 %collective-permute-done.2 = bf16[8,64,512]{2,1,0:T(8,128)(2,1)S(1)} collective-permute-done((bf16[8,64,512]{2,1,0:T(8,128)(2,1)S(1)}, bf16[8,64,512]{2,1,0:T(8,128)(2,1)S(1)}, u32[]{:S(2)}, u32[]{:S(2)}) %collective-permute-start.2) | collective-permute-done | bytes 524320 | tf_op jit(solution)/shard_map/ppermute | solution.py:40
  131.2 0.0 copy-done.2
  131.2 1.3 bitcast_add_fusion
  132.5 5.2 %log_reduce_fusion.3 = (f32[8,512]{1,0:T(8,128)S(1)}, f32[8,128,512]{2,1,0:T(8,128)S(1)}) fusion(f32[8,512,512]{2,1,0:T(8,128)S(1)} %bitcast_add_fusion, f32[8,128]{1,0:T(8,128)S(1)} %get-tuple-element.27, f32[8,128]{1,0:T(8,128)S(1)} %get-tuple-element.23), kind=kLoop, calls=%fused_computation.166 | loop fusion | flops 35123200 | bytes 4218880 | tf_op jit(solution)/shard_map/reduce_sum | solution.py:96
  137.7 7.4 %select_convert_fusion.3 = bf16[8,128,512]{2,1,0:T(8,128)(2,1)S(1)} fusion(f32[8,128,512]{2,1,0:T(8,128)S(1)} %get-tuple-element.14, f32[8,512,512]{2,1,0:T(8,128)S(1)} %fusion.2), kind=kLoop, calls=%fused_computation.236 | loop fusion | flops 44040192 | bytes 5242880 | tf_op jit(solution)/shard_map/convert_element_type | solution.py:93
  145.1 13.3 %log_reduce_fusion.2 = (f32[8,512]{1,0:T(8,128)S(1)}, bf16[8,128,512]{2,1,0:T(8,128)(2,1)S(1)}) fusion(f32[8,512,512]{2,1,0:T(8,128)S(1)} %fusion.2, bf16[8,128,512]{2,1,0:T(8,128)(2,1)S(1)} %select_convert_fusion.3, bf16[8,512,512]{2,1,0:T(8,128)(2,1)S(1)} %bitcast.253, f32[8,512,512]{2,1,0:T(8,128)S(1)} %bitcast_add_fusion, ...), kind=kOutput, calls=%fused_computation.165 | convolution fusion | flops 213905408 | bytes 6578176 | tf_op jit(solution)/shard_map/ipq,iqn->ipn/dot_general | solution.py:86
  158.4 13.5 %log_reduce_fusion.1 = (f32[8,512]{1,0:T(8,128)S(1)}, bf16[8,128,512]{2,1,0:T(8,128)(2,1)S(1)}) fusion(f32[8,512,512]{2,1,0:T(8,128)S(1)} %fusion.2, bf16[8,128,512]{2,1,0:T(8,128)(2,1)S(1)} %get-tuple-element.18, bf16[8,128,512]{2,1,0:T(8,128)(2,1)S(1)} %select_convert_fusion.3, bf16[8,512,512]{2,1,0:T(8,128)(2,1)S(1)} %bitcast.254, ...), kind=kOutput, calls=%fused_computation.164 | convolution fusion | flops 352317440 | bytes 7888896 | tf_op jit(solution)/shard_map/ipq,iqn->ipn/dot_general | solution.py:86
  171.9 0.0 copy-start.1
  171.9 14.6 %log_reduce_fusion = (f32[8,512]{1,0:T(8,128)S(1)}, bf16[8,128,512]{2,1,0:T(8,128)(2,1)}) fusion(f32[8,512,512]{2,1,0:T(8,128)S(1)} %fusion.2, bf16[8,128,512]{2,1,0:T(8,128)(2,1)S(1)} %get-tuple-element.20, bf16[8,128,512]{2,1,0:T(8,128)(2,1)S(1)} %get-tuple-element.18, bf16[8,128,512]{2,1,0:T(8,128)(2,1)S(1)} %select_convert_fusion.3, ...), kind=kOutput, calls=%fused_computation.163 | convolution fusion | flops 491778048 | bytes 9199616 | tf_op jit(solution)/shard_map/ipq,iqn->ipn/dot_general | solution.py:86
  186.5 0.0 copy-done.1
  186.5 0.1 fusion.318
  186.6 44.6 %pmax.7 = f32[8]{0:T(128)S(1)} all-reduce(f32[8]{0:T(128)S(1)} %get-tuple-element.11), channel_id=1, replica_groups=mesh['leaf'=16,'samp'=16] {'samp'}, use_global_device_ids=true, to_apply=%region_5.6 | all-reduce | flops 8 | bytes 64 | tf_op jit(solution)/shard_map/pmax | solution.py:132
  231.2 0.2 fusion.317
  231.4 23.3 %psum.15 = f32[512]{0:T(512)S(1)} all-reduce(f32[512]{0:T(512)S(1)} %get-tuple-element.9), channel_id=1, replica_groups=mesh['leaf'=16,'samp'=16] {'leaf'}, use_global_device_ids=true, to_apply=%region_9.10 | all-reduce | flops 512 | bytes 4096 | tf_op jit(solution)/shard_map/psum | solution.py:135
  254.7 0.6 broadcast_multiply_fusion
  255.3 36.6 %psum.14 = f32[8]{0:T(128)S(1)} all-reduce(f32[8]{0:T(128)S(1)} %get-tuple-element.10), channel_id=1, replica_groups=mesh['leaf'=16,'samp'=16] {'samp'}, use_global_device_ids=true, to_apply=%region_7.8 | all-reduce | flops 8 | bytes 64 | tf_op jit(solution)/shard_map/psum | solution.py:133
  291.9 0.5 multiply_bitcast_fusion
  292.4 4.3 %maximum_bitcast_fusion = bf16[8,1,512,512]{3,2,1,0:T(8,128)(2,1)} fusion(bf16[8,128,512]{2,1,0:T(8,128)(2,1)} %get-tuple-element.22, bf16[8,128,512]{2,1,0:T(8,128)(2,1)} %copy-done.1, bf16[8,128,512]{2,1,0:T(8,128)(2,1)S(1)} %get-tuple-element.18, bf16[8,128,512]{2,1,0:T(8,128)(2,1)S(1)} %select_convert_fusion.3), kind=kLoop, calls=%fused_computation.26 | loop fusion | flops 16777216 | bytes 8388608
  (6 shorter events, 0.1 us)
Async XLA Ops:
  0.6 57.2 %copy-start = (bf16[8,1,512,64]{2,3,1,0:T(8,128)(2,1)S(1)}, bf16[8,1,512,64]{2,3,1,0:T(8,128)(2,1)}, u32[]{:S(2)}) copy-start(bf16[8,1,512,64]{2,3,1,0:T(8,128)(2,1)} %param.12) | copy-start | bytes 1572868
  2.2 12.5 %copy-start.3 = (bf16[8,1,512,512]{3,2,1,0:T(8,128)(2,1)S(1)}, bf16[8,1,512,512]{3,2,1,0:T(8,128)(2,1)}, u32[]{:S(2)}) copy-start(bf16[8,1,512,512]{3,2,1,0:T(8,128)(2,1)} %param.10) | copy-start | bytes 12582916
  41.1 13.6 %copy-start.4 = (bf16[8,1,512,64]{2,3,1,0:T(8,128)(2,1)S(1)}, bf16[8,1,512,64]{2,3,1,0:T(8,128)(2,1)}, u32[]{:S(2)}) copy-start(bf16[8,1,512,64]{2,3,1,0:T(8,128)(2,1)} %param.13) | copy-start | bytes 1572868
  55.7 2.2 collective-permute-start
  98.4 13.7 %copy-start.5 = (bf16[8,1,512,64]{2,3,1,0:T(8,128)(2,1)S(1)}, bf16[8,1,512,64]{2,3,1,0:T(8,128)(2,1)}, u32[]{:S(2)}) copy-start(bf16[8,1,512,64]{2,3,1,0:T(8,128)(2,1)} %param.15) | copy-start | bytes 1572868
  113.4 17.8 %copy-start.2 = (bf16[8,1,512,64]{2,3,1,0:T(8,128)(2,1)S(1)}, bf16[8,1,512,64]{2,3,1,0:T(8,128)(2,1)}, u32[]{:S(2)}) copy-start(bf16[8,1,512,64]{2,3,1,0:T(8,128)(2,1)} %param.14) | copy-start | bytes 1572868
  113.4 2.7 collective-permute-start.1
  116.4 14.8 %collective-permute-start.2 = (bf16[8,64,512]{2,1,0:T(8,128)(2,1)S(1)}, bf16[8,64,512]{2,1,0:T(8,128)(2,1)S(1)}, u32[]{:S(2)}, u32[]{:S(2)}) collective-permute-start(bf16[8,64,512]{2,1,0:T(8,128)(2,1)S(1)} %add_convert_fusion), channel_id=1, source_target_pairs={{0,32},{16,48},{32,0},{48,16},{64,96},{80,112},{96,64},{112,80},{1... | collective-permute-start | bytes 1572872 | tf_op jit(solution)/shard_map/ppermute | solution.py:40
  171.9 14.6 %copy-start.1 = (bf16[8,128,512]{2,1,0:T(8,128)(2,1)}, bf16[8,128,512]{2,1,0:T(8,128)(2,1)S(1)}, u32[]{:S(2)}) copy-start(bf16[8,128,512]{2,1,0:T(8,128)(2,1)S(1)} %get-tuple-element.20) | copy-start | bytes 3145732
where the time goes:
time: 301 us; the launch traced here: 297 us
  matrix products  126 us (42%)
  blocking collectives  105 us (35%)
  other arithmetic  43.9 us (15%)
  waiting for transfers between devices  16.6 us (6%)
  starting transfers between devices  3.04 us (1%)
    dot_general x9, matrix products, leaf_pass(): jnp.einsum('ipq,iqn->ipn', lower_loc[:, row_begin:row_end, :row_begin], e...  121 us
    pmax x1, blocking collectives, per_device(): peak = lax.pmax(local_peak, 'samp')  44.6 us
    psum x1, blocking collectives, per_device(): mass = lax.psum(jnp.sum(jnp.exp(logsum - peak[:, None]), axis=1), 'samp')  36.6 us
    convert_element_type x3, other arithmetic, leaf_pass(): normal_quantile(points[:, row_begin:row_end] * normal_cdf(scaled))  28.5 us
    psum x1, blocking collectives, per_device(): sample_total_log = lax.psum(sample_sums, 'leaf')  23.3 us
    ppermute x3, waiting for transfers between devices, partner(): lax.ppermute(array, axis, [(i, i ^ 1 << distance) for i in range(lax.axis...  16.6 us
  transfers between devices with their start and end apart: 3, of which 3 were waited for; matrix products, arithmetic and copies ran while one was open for 0% of the time, Pallas kernels for 0%

commit v1 on v0

v1 whole, which is shorter than its diff:
```python
import functools
import math

import jax
import jax.numpy as jnp
from jax import lax
from jax.experimental import pallas as pl
from jax.experimental.pallas import tpu as pltpu
from jax.sharding import PartitionSpec as P

LEAVES = 8
M = 512
R = 64
SUB = 128
COLS = 512
HALF = 256
CHUNK = 16
TOTAL = 8192
MESH = pl.DeviceIdType.MESH

coef_a = (
    -39.69683028665376,
    220.9460984245205,
    -275.9285104469687,
    138.357751867269,
    -30.66479806614716,
    2.506628277459239,
)
coef_b = (
    -54.47609879822406,
    161.5858368580409,
    -155.6989798598866,
    66.80131188771972,
    -13.28068155288572,
    1.0,
)
coef_c = (
    -0.007784894002430293,
    -0.3223964580411365,
    -2.400758277161838,
    -2.549732539343734,
    4.374664141464968,
    2.938163982698783,
)
coef_d = (0.007784695709041462, 0.3224671290700398, 2.445134137142996, 3.754408661907416, 1.0)
split_low = 0.02425

K = coef_a[0] / coef_b[0]
G = math.sqrt(2.0 * math.log(2.0))
TAIL = -coef_c[0] * G / coef_d[0]
mono_a = tuple(v / coef_a[0] * K ** (2 * j) for j, v in enumerate(coef_a))
mono_b = tuple(v / coef_b[0] * K ** (2 * j) for j, v in enumerate(coef_b))
mono_c = tuple(v / coef_c[0] * G**-j for j, v in enumerate(coef_c))
mono_d = tuple(v / coef_d[0] * G**-j for j, v in enumerate(coef_d))

ROOT_HALF = math.sqrt(0.5)
FLOOR = -6.0 * ROOT_HALF
ERFC_FROM = -3.0 * ROOT_HALF
erfc_log2 = (
    0.0003123880466,
    0.00671664281,
    0.06322885333,
    -1.09054892,
    1.442791442,
    -0.08385716881,
)


def twice_cdf(z):
    tail = jnp.full_like(z, erfc_log2[0])
    tail = z * erfc_log2[0] + erfc_log2[1]
    for entry in erfc_log2[2:]:
        tail = tail * z + entry
    return jnp.where(z < ERFC_FROM, lax.exp2(tail), lax.erf(z) + 1.0)


def quantile(p):
    centre = p - 0.5 * K
    square = centre * centre
    small = jnp.minimum(p, K - p)
    tail = small < K * split_low
    depth = math.log2(K) - jnp.log2(small)
    depth = depth * lax.rsqrt(depth)
    var = jnp.where(tail, depth, square)
    top = var + jnp.where(tail, mono_c[1], mono_a[1])
    for c, a in zip(mono_c[2:], mono_a[2:]):
        top = top * var + jnp.where(tail, c, a)
    low = jnp.where(tail, 1.0, square + mono_b[1])
    for d, b in zip(mono_d[1:], mono_b[2:]):
        low = low * var + jnp.where(tail, d, b)
    scale = jnp.where(tail, jnp.where(centre < 0.0, -TAIL, TAIL), centre)
    return scale * top / low


def kernel(
    limits,
    scales,
    lower_hbm,
    gens,
    col_one_hbm,
    row_one_hbm,
    col_two_hbm,
    row_two_hbm,
    draws_hbm,
    mean_out,
    sample_out,
    lower,
    col_one,
    row_one,
    col_two,
    row_two,
    points,
    limit_b,
    scale_b,
    acc_0,
    acc_1,
    draw_0,
    draw_1,
    log_0,
    log_1,
    first_send,
    first_recv,
    second_send,
    second_recv,
    pair_send,
    pair_recv,
    stat_all,
    sums_all,
    load_sem,
    out_sem,
    first_sems,
    second_sems,
    pair_sems,
    stat_sems,
    sums_sems,
):
    leaf = lax.axis_index("leaf")
    samp = lax.axis_index("samp")
    n_leaf = lax.axis_size("leaf")
    n_samp = lax.axis_size("samp")
    sibling = leaf + 1 - 2 * lax.rem(leaf, 2)
    across = leaf + 2 - 4 * lax.rem(leaf // 2, 2)
    acc = (acc_0, acc_1)
    draw = (draw_0, draw_1)
    log_sum = (log_0, log_1)

    loads = (
        (lower_hbm, lower),
        (col_one_hbm, col_one),
        (row_one_hbm, row_one),
        (col_two_hbm, col_two),
        (row_two_hbm, row_two),
    )

    def load(which, i):
        src, dst = loads[which]
        return pltpu.make_async_copy(src.at[i, 0], dst.at[i], load_sem.at[which, i])

    def start_loads(which):
        def body(i, carry):
            load(which, i).start()
            return carry

        lax.fori_loop(0, LEAVES, body, 0)

    start_loads(0)
    start_loads(2)
    start_loads(1)
    start_loads(4)
    start_loads(3)

    barrier = pltpu.get_barrier_semaphore()

    def greet_leaf(d, carry):
        pl.semaphore_signal(
            barrier, inc=1, device_id={"leaf": lax.rem(leaf + d, n_leaf)}, device_id_type=MESH
        )
        return carry

    def greet_samp(d, carry):
        pl.semaphore_signal(
            barrier, inc=1, device_id={"samp": lax.rem(samp + d, n_samp)}, device_id_type=MESH
        )
        return carry

    lax.fori_loop(1, n_leaf, greet_leaf, 0)
    lax.fori_loop(1, n_samp, greet_samp, 0)

    def first_copy(i):
        return pltpu.make_async_remote_copy(
            src_ref=first_send.at[i],
            dst_ref=first_recv.at[i],
            send_sem=first_sems.at[0, i],
            recv_sem=first_sems.at[1, i],
            device_id={"leaf": sibling},
            device_id_type=MESH,
        )

    def second_copy(i):
        return pltpu.make_async_remote_copy(
            src_ref=second_send.at[i],
            dst_ref=second_recv.at[i],
            send_sem=second_sems.at[0, i],
            recv_sem=second_sems.at[1, i],
            device_id={"leaf": sibling},
            device_id_type=MESH,
        )

    def pair_copy(i):
        return pltpu.make_async_remote_copy(
            src_ref=pair_send.at[i],
            dst_ref=pair_recv.at[i],
            send_sem=pair_sems.at[0, i],
            recv_sem=pair_sems.at[1, i],
            device_id={"leaf": across},
            device_id_type=MESH,
        )

    def out_copy(i, h):
        return pltpu.make_async_copy(
            draw[h].at[lax.rem(i, 2)],
            draws_hbm.at[i, 0, :, pl.ds(h * HALF, HALF)],
            out_sem.at[h, i],
        )

    def spread(row):
        return jnp.broadcast_to(row, (SUB, SUB)).T

    def product(step, i, s, h):
        rows = slice(s * SUB, (s + 1) * SUB)
        cols = slice(h * HALF, (h + 1) * HALF)
        left, right = [], []
        if step > 0:
            left.append(
                jnp.concatenate([col_one[i, rows, :], col_two[i, rows, :]], axis=1)
            )
            right.append(first_recv[i, :, cols])
            if step == 1:
                right.append(jnp.zeros((R, HALF), jnp.bfloat16))
            else:
                right.append(pair_recv[i, :, cols])
        if s > 0:
            left.append(lower[i, rows, : s * SUB])
            right.append(draw[h][lax.rem(i, 2), : s * SUB, :])
        if not left:
            return
        a = left[0] if len(left) == 1 else jnp.concatenate(left, axis=1)
        b = right[0] if len(right) == 1 else jnp.concatenate(right, axis=0)
        acc[h][...] = jnp.dot(a, b, preferred_element_type=jnp.float32)

    def elementwise(step, i, s, h, gen_b):
        par = lax.rem(i, 2)
        total = None
        group = []
        for chunk in range(SUB // CHUNK):
            at = s * SUB + chunk * CHUNK
            rows = slice(at, at + CHUNK)
            cols = slice(h * HALF, (h + 1) * HALF)
            here = slice(chunk * CHUNK, (chunk + 1) * CHUNK)
            limit = limit_b[i, rows, :]
            scale = scale_b[i, rows, :]
            if step == 0 and s == 0:
                y = twice_cdf(jnp.maximum(scale * limit, FLOOR))
                y = jnp.concatenate([y, y], axis=1)
            else:
                limit = jnp.concatenate([limit, limit], axis=1)
                scale = jnp.concatenate([scale, scale], axis=1)
                z = jnp.maximum(scale * (limit - acc[h][here, :]), FLOOR)
                y = twice_cdf(z)
            if step == 0:
                g = gen_b[here, :]
                g = jnp.concatenate([g, g], axis=1)
                n = (
                    lax.broadcasted_iota(jnp.int32, (CHUNK, HALF), 1)
                    + (samp * COLS + h * HALF)
                )
                residue = jnp.bitwise_and(g * n, TOTAL - 1).astype(jnp.float32)
                u = residue * (0.5 * K / TOTAL) + 0.25 * K / TOTAL
                points[i, rows, cols] = u
            else:
                u = points[i, rows, cols]
            draw[h][par, rows, :] = quantile(u * y).astype(jnp.bfloat16)
            if step == 2:
                group.append(y[:8] * y[8:])
                if len(group) == 2:
                    term = jnp.log2(group[0] * group[1])
                    total = term if total is None else total + term
                    group = []
        if step == 2:
            if s == 0:
                log_sum[h][i] = total
            else:
                log_sum[h][i] += total

    units = [(s, h) for s in range(M // SUB) for h in range(2)]

    def leaf_pass(step, i, hooks):
        for at, (s, h) in enumerate(units):
            if at in hooks:
                hooks[at]()
            if at + 1 < len(units):
                product(step, i, *units[at + 1])
            gen_b = None
            if step == 0:
                row = gens[i, :, s * SUB : (s + 1) * SUB].astype(jnp.float32)
                gen_b = spread(row).astype(jnp.int32)
            elementwise(step, i, s, h, gen_b)

    def contract(basis, i):
        par = lax.rem(i, 2)
        both = jnp.concatenate([draw_0[par], draw_1[par]], axis=1)
        return lax.dot_general(
            basis[i], both, (((0,), (0,)), ((), ())), preferred_element_type=jnp.float32
        )

    def pass_a(i, carry):
        for s in range(M // SUB):
            cols = slice(s * SUB, (s + 1) * SUB)
            limit_b[i, cols, :] = spread(limits[i, :, cols])
            scale_b[i, cols, :] = spread(scales[i, :, cols] * ROOT_HALF)
        load(0, i).wait()
        load(2, i).wait()

        def send():
            @pl.when(i == 1)
            def _():
                pl.semaphore_wait(barrier, n_leaf + n_samp - 2)

            @pl.when(i >= 1)
            def _():
                first_copy(i - 1).start()

        leaf_pass(0, i, {2: send})
        first_send[i] = contract(row_one, i).astype(jnp.bfloat16)
        return carry

    lax.fori_loop(0, LEAVES, pass_a, 0)

    def pass_b(i, carry):
        load(1, i).wait()
        load(3, i).wait()
        load(4, i).wait()
        first_copy(i).wait_recv()

        def send():
            @pl.when(i == 0)
            def _():
                first_copy(LEAVES - 1).start()

            @pl.when(i >= 1)
            def _():
                second_copy(i - 1).start()

        def pair():
            @pl.when(i >= 2)
            def _():
                add_pair(i - 2)

        def send_pair():
            @pl.when(i >= 2)
            def _():
                pair_copy(i - 2).start()

        product(1, i, *units[0])
        leaf_pass(1, i, {1: pair, 2: send, 3: send_pair})
        second_send[i] = contract(row_two, i)
        return carry

    def add_pair(i):
        second_copy(i).wait_recv()
        pair_send[i] = (second_send[i] + second_recv[i]).astype(jnp.bfloat16)

    lax.fori_loop(0, LEAVES, pass_b, 0)

    def pass_c(i, carry):
        pair_copy(i).wait_recv()

        @pl.when(i >= 2)
        def _():
            out_copy(i - 2, 0).wait()
            out_copy(i - 2, 1).wait()

        def send():
            @pl.when(i == 0)
            def _():
                second_copy(LEAVES - 1).start()

        def pair():
            @pl.when(i < 2)
            def _():
                add_pair(i + LEAVES - 2)

        def send_pair():
            @pl.when(i < 2)
            def _():
                pair_copy(i + LEAVES - 2).start()

        product(2, i, *units[0])
        leaf_pass(2, i, {1: pair, 2: send, 3: send_pair})
        out_copy(i, 0).start()
        out_copy(i, 1).start()
        return carry

    lax.fori_loop(0, LEAVES, pass_c, 0)

    logsum = jnp.concatenate(
        [jnp.sum(log_0[...], axis=1), jnp.sum(log_1[...], axis=1)], axis=1
    )
    logsum = (logsum - float(M)) * math.log(2.0)
    peak = jnp.max(logsum, axis=1, keepdims=True)
    mass = jnp.sum(jnp.exp(logsum - peak), axis=1, keepdims=True)
    lane = lax.broadcasted_iota(jnp.int32, (LEAVES, SUB), 1)
    stat_all[samp] = jnp.where(lane == 0, peak, mass)
    sums_all[leaf] = jnp.sum(logsum, axis=0, keepdims=True)

    def stat_copy(d):
        to = lax.rem(samp + d, n_samp)
        return pltpu.make_async_remote_copy(
            src_ref=stat_all.at[samp],
            dst_ref=stat_all.at[samp],
            send_sem=stat_sems.at[0, d],
            recv_sem=stat_sems.at[1, d],
            device_id={"samp": to},
            device_id_type=MESH,
        )

    def sums_copy(d):
        to = lax.rem(leaf + d, n_leaf)
        return pltpu.make_async_remote_copy(
            src_ref=sums_all.at[leaf],
            dst_ref=sums_all.at[leaf],
            send_sem=sums_sems.at[0, d],
            recv_sem=sums_sems.at[1, d],
            device_id={"leaf": to},
            device_id_type=MESH,
        )

    def each(copy, what, count):
        def body(d, carry):
            what(copy(d))
            return carry

        lax.fori_loop(1, count, body, 0)

    each(stat_copy, lambda c: c.start(), n_samp)
    each(sums_copy, lambda c: c.start(), n_leaf)

    def drain(i, carry):
        first_copy(i).wait_send()
        second_copy(i).wait_send()
        pair_copy(i).wait_send()
        return carry

    lax.fori_loop(0, LEAVES, drain, 0)
    for i in (LEAVES - 2, LEAVES - 1):
        out_copy(i, 0).wait()
        out_copy(i, 1).wait()
    each(stat_copy, lambda c: c.wait(), n_samp)
    each(sums_copy, lambda c: c.wait(), n_leaf)

    stats = stat_all[...]
    peaks = stats[:, :, 0:1]
    top = jnp.max(peaks, axis=0)
    whole = jnp.sum(stats[:, :, 1:2] * jnp.exp(peaks - top[None]), axis=0)
    mean_out[...] = (top + jnp.log(whole / TOTAL)) / M
    sample_out[...] = jnp.sum(sums_all[...], axis=0) / (LEAVES * n_leaf * M)


def per_device(limits, inv_scale, lower_blocks, qmc_gen, col_one, row_one, col_two, row_two):
    vmem = pl.BlockSpec(memory_space=pltpu.VMEM)
    anywhere = pl.BlockSpec(memory_space=pl.ANY)
    f32, bf16 = jnp.float32, jnp.bfloat16
    n_leaf, n_samp = lax.axis_size("leaf"), lax.axis_size("samp")
    dma = pltpu.SemaphoreType.DMA
    draws, mean_log, sample_log = pl.pallas_call(
        kernel,
        out_shape=(
            jax.ShapeDtypeStruct((LEAVES, 1, M, COLS), bf16),
            jax.ShapeDtypeStruct((LEAVES, 1), f32),
            jax.ShapeDtypeStruct((1, COLS), f32),
        ),
        in_specs=[vmem, vmem, anywhere, vmem, anywhere, anywhere, anywhere, anywhere],
        out_specs=(anywhere, vmem, vmem),
        scratch_shapes=[
            pltpu.VMEM((LEAVES, M, M), bf16),
            pltpu.VMEM((LEAVES, M, R), bf16),
            pltpu.VMEM((LEAVES, M, R), bf16),
            pltpu.VMEM((LEAVES, M, R), bf16),
            pltpu.VMEM((LEAVES, M, R), bf16),
            pltpu.VMEM((LEAVES, M, COLS), f32),
            pltpu.VMEM((LEAVES, M, SUB), f32),
            pltpu.VMEM((LEAVES, M, SUB), f32),
            pltpu.VMEM((SUB, HALF), f32),
            pltpu.VMEM((SUB, HALF), f32),
            pltpu.VMEM((2, M, HALF), bf16),
            pltpu.VMEM((2, M, HALF), bf16),
            pltpu.VMEM((LEAVES, 8, HALF), f32),
            pltpu.VMEM((LEAVES, 8, HALF), f32),
            pltpu.VMEM((LEAVES, R, COLS), bf16),
            pltpu.VMEM((LEAVES, R, COLS), bf16),
            pltpu.VMEM((LEAVES, R, COLS), f32),
            pltpu.VMEM((LEAVES, R, COLS), f32),
            pltpu.VMEM((LEAVES, R, COLS), bf16),
            pltpu.VMEM((LEAVES, R, COLS), bf16),
            pltpu.VMEM((n_samp, LEAVES, SUB), f32),
            pltpu.VMEM((n_leaf, 1, COLS), f32),
            dma((5, LEAVES)),
            dma((2, LEAVES)),
            dma((2, LEAVES)),
            dma((2, LEAVES)),
            dma((2, LEAVES)),
            dma((2, n_samp)),
            dma((2, n_leaf)),
        ],
        compiler_params=pltpu.CompilerParams(
            collective_id=0, has_side_effects=True, vmem_limit_bytes=60 * 1024 * 1024
        ),
        name="conditioning",
    )(limits, inv_scale, lower_blocks, qmc_gen, col_one, row_one, col_two, row_two)
    return draws, mean_log, sample_log[0]


def solution(mesh):
    return jax.shard_map(
        per_device,
        mesh=mesh,
        in_specs=(
            P(None, "leaf", None),
            P(None, "leaf", None),
            P(None, "leaf", None, None),
            P(None, "leaf", None),
            P(None, "leaf", None, None),
            P(None, "leaf", None, None),
            P(None, "leaf", None, None),
            P(None, "leaf", None, None),
        ),
        out_specs=(P(None, "leaf", None, "samp"), P(None, "leaf"), P("samp")),
        check_vma=False,
    )
```

time: 301 us -> 106 us (0.35); the launches traced: 297 us -> 106 us
  matrix products: 126 us -> 0 us
  blocking collectives: 105 us -> 0 us
  Pallas kernels: 0 us -> 90.4 us
  other arithmetic: 43.9 us -> 0 us
  waiting for transfers between devices: 16.6 us -> 0 us
  local copies, waits for them, and re-layouts: 1.56 us -> 14.8 us
  starting transfers between devices: 3.04 us -> 0 us
    dot_general x13 -> x0, matrix products: 126 us -> none  [the longest x9 121 us: leaf_pass(): jnp.einsum('ipq,iqn->ipn', lower_loc[:, row_begin:row_end, :row_begin], e...]
    pallas_call x0 -> x1, Pallas kernels: none -> 90.4 us  [per_device(): pl.pallas_call(kernel, out_shape=(jax.ShapeDtypeStruct((LEAVES, 1, M, COL...]
    psum x2 -> x0, blocking collectives: 59.9 us -> none  [the longest x1 36.6 us: per_device(): mass = lax.psum(jnp.sum(jnp.exp(logsum - peak[:, None]), axis=1), 'samp')]
    pmax x1 -> x0, blocking collectives: 44.6 us -> none  [per_device(): peak = lax.pmax(local_peak, 'samp')]
    convert_element_type x4 -> x0, other arithmetic: 28.7 us -> none  [the longest x3 28.5 us: leaf_pass(): normal_quantile(points[:, row_begin:row_end] * normal_cdf(scaled))]
    ppermute x3 -> x0, waiting for transfers between devices: 16.6 us -> none  [partner(): lax.ppermute(array, axis, [(i, i ^ 1 << distance) for i in range(lax.axis...]
    unnamed x14 -> x11, local copies, waits for them, and re-layouts: 1.55 us -> 14.8 us
    reduce_sum x2 -> x0, other arithmetic: 5.4 us -> none  [the longest x1 5.21 us: leaf_pass(): logsum = logsum + jnp.sum(log_normal_cdf(scaled), axis=1)]
  transfers between devices with their start and end apart: 3 -> 0, of which waited for: 3 -> 0; matrix products, arithmetic and copies ran while one was open for 0% -> 0% of each run, Pallas kernels for 0% -> 0%
where the time goes in v1:
time: 106 us
  Pallas kernels  90.4 us (85%)
  local copies, waits for them, and re-layouts  14.8 us (14%)
    pallas_call x1, Pallas kernels, per_device(): pl.pallas_call(kernel, out_shape=(jax.ShapeDtypeStruct((LEAVES, 1, M, COL...  90.4 us
    unnamed x11, local copies, waits for them, and re-layouts  14.8 us

profile of v1, /device:TPU:2, one launch (start us, length us, event | category | flops | bytes accessed | tf_op | source)
XLA Modules:
  0.0 105.9 jit_solution(6303147925357227200)
XLA Ops:
  0.6 0.0 copy-start
  0.6 2.4 %copy.11.col_one_hbm = bf16[8,1,512,64]{3,2,1,0:T(8,128)(2,1)} copy(bf16[8,1,512,64]{2,3,1,0:T(8,128)(2,1)} %param.12) | data formatting | bytes 1048576 | tf_op args[4]
  3.1 2.4 %copy.12.row_one_hbm = bf16[8,1,512,64]{3,2,1,0:T(8,128)(2,1)} copy(bf16[8,1,512,64]{2,3,1,0:T(8,128)(2,1)} %param.13) | data formatting | bytes 1048576 | tf_op args[5]
  5.4 2.4 %copy.13.col_two_hbm = bf16[8,1,512,64]{3,2,1,0:T(8,128)(2,1)} copy(bf16[8,1,512,64]{2,3,1,0:T(8,128)(2,1)} %param.14) | data formatting | bytes 1048576 | tf_op args[6]
  7.8 0.0 copy-done
  7.8 1.3 %copy.14.row_two_hbm = bf16[8,1,512,64]{3,2,1,0:T(8,128)(2,1)} copy(bf16[8,1,512,64]{2,3,1,0:T(8,128)(2,1)S(1)} %copy-done) | data formatting | bytes 1048576 | tf_op args[7]
  9.2 90.4 %conditioning.1 = (bf16[8,1,512,512]{3,2,1,0:T(8,128)(2,1)}, f32[8,1]{1,0:T(8,128)}, f32[1,512]{1,0:T(1,128)}) custom-call(f32[8,1,512]{2,1,0:T(1,128)} %limits.1, f32[8,1,512]{2,1,0:T(1,128)} %scales.1, bf16[8,1,512,512]{3,2,1,0:T(8,128)(2,1)} %lower_hbm.1, s32[8,1,512]{2,1,0:T(1,128)} %gens.1, bf16[8,1,512,64]{3,2,1,0:T(8,128)(2,1)} %copy.11.col_one_hbm, ...), custom_call_target="tpu_custom_call" | custom-call | tf_op jit(solution)/shard_map/conditioning/pallas_call | solution.py:475
  99.6 1.3 %copy.15 = f32[8,1]{0,1:T(1,128)} copy(f32[8,1]{1,0:T(8,128)} %get-tuple-element.10) | data formatting | bytes 64
  100.8 0.0 copy-start.1
  100.8 4.5 %copy.18 = bf16[8,1,512,512]{3,2,1,0:T(8,128)(2,1)} copy(bf16[8,1,512,512]{3,2,1,0:T(8,128)(2,1)} %get-tuple-element.15) | data formatting | bytes 8388608
  105.3 0.0 copy-done.1
  105.3 0.6 copy.19
Async XLA Ops:
  0.6 7.2 %copy-start = (bf16[8,1,512,64]{2,3,1,0:T(8,128)(2,1)S(1)}, bf16[8,1,512,64]{2,3,1,0:T(8,128)(2,1)}, u32[]{:S(2)}) copy-start(bf16[8,1,512,64]{2,3,1,0:T(8,128)(2,1)} %param.15) | copy-start | bytes 1572868
  100.8 4.5 %copy-start.1 = (f32[1,512]{1,0:T(1,128)S(1)}, f32[1,512]{1,0:T(1,128)}, u32[]{:S(2)}) copy-start(f32[1,512]{1,0:T(1,128)} %get-tuple-element.8) | copy-start | bytes 6148

commit v2 on v1

--- a/solution.py
+++ b/solution.py
@@ -47,34 +47,34 @@
 
 K = coef_a[0] / coef_b[0]
 G = math.sqrt(2.0 * math.log(2.0))
+EDGE = K * (0.5 - split_low)
 TAIL = -coef_c[0] * G / coef_d[0]
 mono_a = tuple(v / coef_a[0] * K ** (2 * j) for j, v in enumerate(coef_a))
 mono_b = tuple(v / coef_b[0] * K ** (2 * j) for j, v in enumerate(coef_b))
 mono_c = tuple(v / coef_c[0] * G**-j for j, v in enumerate(coef_c))
-mono_d = tuple(v / coef_d[0] * G**-j for j, v in enumerate(coef_d))
+mono_d = tuple(EDGE / TAIL * v / coef_d[0] * G**-j for j, v in enumerate(coef_d))
 
 ROOT_HALF = math.sqrt(0.5)
 FLOOR = -6.0 * ROOT_HALF
-ERFC_FROM = -3.0 * ROOT_HALF
+ERFC_FROM = -3.5 * ROOT_HALF
 erfc_log2 = (
-    0.0003123880466,
-    0.00671664281,
-    0.06322885333,
-    -1.09054892,
-    1.442791442,
-    -0.08385716881,
+    0.001479457231,
+    0.02841664334,
+    -1.205206352,
+    1.255708033,
+    -0.2048280003,
 )
 
 
 def twice_cdf(z):
-    tail = jnp.full_like(z, erfc_log2[0])
     tail = z * erfc_log2[0] + erfc_log2[1]
     for entry in erfc_log2[2:]:
         tail = tail * z + entry
     return jnp.where(z < ERFC_FROM, lax.exp2(tail), lax.erf(z) + 1.0)
 
 
-def quantile(p):
+def quantile(p, centre_coefs):
+    mono = [tile(c, p.shape) for c in centre_coefs]
     centre = p - 0.5 * K
     square = centre * centre
     small = jnp.minimum(p, K - p)
@@ -82,14 +82,19 @@
     depth = math.log2(K) - jnp.log2(small)
     depth = depth * lax.rsqrt(depth)
     var = jnp.where(tail, depth, square)
-    top = var + jnp.where(tail, mono_c[1], mono_a[1])
-    for c, a in zip(mono_c[2:], mono_a[2:]):
+    top = var + jnp.where(tail, mono_c[1], mono[0])
+    for c, a in zip(mono_c[2:], mono[1:5]):
         top = top * var + jnp.where(tail, c, a)
-    low = jnp.where(tail, 1.0, square + mono_b[1])
-    for d, b in zip(mono_d[1:], mono_b[2:]):
+    low = jnp.where(tail, mono_d[0], square + mono_b[1])
+    for d, b in zip(mono_d[1:], mono[5:]):
         low = low * var + jnp.where(tail, d, b)
-    scale = jnp.where(tail, jnp.where(centre < 0.0, -TAIL, TAIL), centre)
+    scale = jnp.clip(centre, -EDGE, EDGE)
     return scale * top / low
+
+
+def tile(block, shape):
+    block = jnp.concatenate([block] * (shape[1] // 128), axis=1)
+    return jnp.concatenate([block] * (shape[0] // 8), axis=0)
 
 
 def kernel(
@@ -105,12 +110,14 @@
     mean_out,
     sample_out,
     lower,
-    col_one,
+    cols_t,
     row_one,
-    col_two,
     row_two,
+    cols_b,
+    cols_c,
+    tops,
+    table,
     points,
-    limit_b,
     scale_b,
     acc_0,
     acc_1,
@@ -146,15 +153,20 @@
 
     loads = (
         (lower_hbm, lower),
-        (col_one_hbm, col_one),
         (row_one_hbm, row_one),
-        (col_two_hbm, col_two),
         (row_two_hbm, row_two),
+        (col_one_hbm, cols_t),
+        (col_two_hbm, cols_t),
     )
 
     def load(which, i):
         src, dst = loads[which]
-        return pltpu.make_async_copy(src.at[i, 0], dst.at[i], load_sem.at[which, i])
+        dst = dst.at[i]
+        if which == 3:
+            dst = dst.at[:R]
+        if which == 4:
+            dst = dst.at[R:]
+        return pltpu.make_async_copy(src.at[i, 0], dst, load_sem.at[which, i])
 
     def start_loads(which):
         def body(i, carry):
@@ -163,11 +175,14 @@
 
         lax.fori_loop(0, LEAVES, body, 0)
 
-    start_loads(0)
-    start_loads(2)
-    start_loads(1)
-    start_loads(4)
-    start_loads(3)
+    for which in (0, 3, 4, 1, 2):
+        start_loads(which)
+    for at, value in enumerate(mono_a[1:] + mono_b[2:]):
+        table[at] = jnp.full((8, 128), value, jnp.float32)
+    for h in range(2):
+        draw[h][1] = jnp.zeros((M, HALF), jnp.bfloat16)
+    row = lax.broadcasted_iota(jnp.int32, (SUB, HALF), 0)
+    ones_row = jnp.where(row < 3, 1.0, 0.0).astype(jnp.bfloat16)
 
     barrier = pltpu.get_barrier_semaphore()
 
@@ -230,25 +245,23 @@
         rows = slice(s * SUB, (s + 1) * SUB)
         cols = slice(h * HALF, (h + 1) * HALF)
         left, right = [], []
-        if step > 0:
-            left.append(
-                jnp.concatenate([col_one[i, rows, :], col_two[i, rows, :]], axis=1)
-            )
-            right.append(first_recv[i, :, cols])
-            if step == 1:
-                right.append(jnp.zeros((R, HALF), jnp.bfloat16))
-            else:
-                right.append(pair_recv[i, :, cols])
+        if step == 1:
+            left.append(cols_b[i, rows, :])
+            right += [first_recv[i, :, cols], ones_row[:R]]
+        if step == 2:
+            left.append(cols_c[i, rows, :])
+            right += [first_recv[i, :, cols], pair_recv[i, :, cols]]
+        if step != 1:
+            left.append(tops[i, rows, :])
+            right.append(ones_row)
         if s > 0:
             left.append(lower[i, rows, : s * SUB])
             right.append(draw[h][lax.rem(i, 2), : s * SUB, :])
-        if not left:
-            return
         a = left[0] if len(left) == 1 else jnp.concatenate(left, axis=1)
         b = right[0] if len(right) == 1 else jnp.concatenate(right, axis=0)
         acc[h][...] = jnp.dot(a, b, preferred_element_type=jnp.float32)
 
-    def elementwise(step, i, s, h, gen_b):
+    def elementwise(step, i, s, h, gen_b, limit_0):
         par = lax.rem(i, 2)
         total = None
         group = []
@@ -257,16 +270,13 @@
             rows = slice(at, at + CHUNK)
             cols = slice(h * HALF, (h + 1) * HALF)
             here = slice(chunk * CHUNK, (chunk + 1) * CHUNK)
-            limit = limit_b[i, rows, :]
             scale = scale_b[i, rows, :]
             if step == 0 and s == 0:
-                y = twice_cdf(jnp.maximum(scale * limit, FLOOR))
+                y = twice_cdf(jnp.maximum(scale * limit_0[here, :], FLOOR))
                 y = jnp.concatenate([y, y], axis=1)
             else:
-                limit = jnp.concatenate([limit, limit], axis=1)
                 scale = jnp.concatenate([scale, scale], axis=1)
-                z = jnp.maximum(scale * (limit - acc[h][here, :]), FLOOR)
-                y = twice_cdf(z)
+                y = twice_cdf(jnp.maximum(scale * acc[h][here, :], FLOOR))
             if step == 0:
                 g = gen_b[here, :]
                 g = jnp.concatenate([g, g], axis=1)
@@ -279,7 +289,8 @@
                 points[i, rows, cols] = u
             else:
                 u = points[i, rows, cols]
-            draw[h][par, rows, :] = quantile(u * y).astype(jnp.bfloat16)
+            coefs = [table[j] for j in range(9)]
+            draw[h][par, rows, :] = quantile(u * y, coefs).astype(jnp.bfloat16)
             if step == 2:
                 group.append(y[:8] * y[8:])
                 if len(group) == 2:
@@ -294,32 +305,58 @@
 
     units = [(s, h) for s in range(M // SUB) for h in range(2)]
 
-    def leaf_pass(step, i, hooks):
+    def leaf_pass(step, i, hooks, limit_0=None):
+        gen_b = None
         for at, (s, h) in enumerate(units):
             if at in hooks:
                 hooks[at]()
             if at + 1 < len(units):
-                product(step, i, *units[at + 1])
-            gen_b = None
-            if step == 0:
+                if step > 0 or units[at + 1][0] > 0:
+                    product(step, i, *units[at + 1])
+            elif step > 0:
+                product(step, jnp.minimum(i + 1, LEAVES - 1), *units[0])
+            if step == 0 and h == 0:
                 row = gens[i, :, s * SUB : (s + 1) * SUB].astype(jnp.float32)
                 gen_b = spread(row).astype(jnp.int32)
-            elementwise(step, i, s, h, gen_b)
-
-    def contract(basis, i):
-        par = lax.rem(i, 2)
+            elementwise(step, i, s, h, gen_b, limit_0)
+
+    def contract(basis, i, par):
         both = jnp.concatenate([draw_0[par], draw_1[par]], axis=1)
-        return lax.dot_general(
-            basis[i], both, (((0,), (0,)), ((), ())), preferred_element_type=jnp.float32
-        )
+        return jnp.dot(basis[i], both, preferred_element_type=jnp.float32)
+
+    def first_coef(i, par):
+        first_send[i] = contract(row_one, i, par).astype(jnp.bfloat16)
+
+    def second_coef(i, par):
+        second_send[i] = contract(row_two, i, par)
+
+    last = LEAVES - 1
 
     def pass_a(i, carry):
+        for which in (0, 1, 3, 4):
+            load(which, i).wait()
+        before = jnp.maximum(i - 1, 0)
+        first_coef(before, lax.rem(i + 1, 2))
+        limit = -limits[i]
+        high = limit.astype(jnp.bfloat16)
+        rest = limit - high.astype(jnp.float32)
+        mid = rest.astype(jnp.bfloat16)
+        tiny = (rest - mid.astype(jnp.float32)).astype(jnp.bfloat16)
+        at = lax.broadcasted_iota(jnp.int32, (SUB, SUB), 0)
+        limit_0 = spread(limit[:, :SUB])
         for s in range(M // SUB):
-            cols = slice(s * SUB, (s + 1) * SUB)
-            limit_b[i, cols, :] = spread(limits[i, :, cols])
-            scale_b[i, cols, :] = spread(scales[i, :, cols] * ROOT_HALF)
-        load(0, i).wait()
-        load(2, i).wait()
+            rows = slice(s * SUB, (s + 1) * SUB)
+            scale_b[i, rows, :] = spread(scales[i, :, rows] * -ROOT_HALF)
+            parts = [
+                jnp.broadcast_to(v[:, rows].astype(jnp.float32), (SUB, SUB))
+                for v in (high, mid, tiny)
+            ]
+            part = jnp.where(at == 0, parts[0], jnp.where(at == 1, parts[1], parts[2]))
+            part = jnp.where(at < 3, part, 0.0).astype(jnp.bfloat16)
+            tops[i, rows, :] = part.T
+            pair = cols_t[i, :, rows]
+            cols_c[i, rows, :] = pair.T
+            cols_b[i, rows, :] = jnp.concatenate([pair[:R], part[:R]], axis=0).T
 
         def send():
             @pl.when(i == 1)
@@ -330,22 +367,27 @@
             def _():
                 first_copy(i - 1).start()
 
-        leaf_pass(0, i, {2: send})
-        first_send[i] = contract(row_one, i).astype(jnp.bfloat16)
+        leaf_pass(0, i, {2: send}, limit_0)
         return carry
 
     lax.fori_loop(0, LEAVES, pass_a, 0)
+    first_coef(last, last % 2)
+    first_copy(0).wait_recv()
+    product(1, 0, *units[0])
 
     def pass_b(i, carry):
-        load(1, i).wait()
-        load(3, i).wait()
-        load(4, i).wait()
-        first_copy(i).wait_recv()
+        load(2, i).wait()
+
+        @pl.when(i < last)
+        def _():
+            first_copy(i + 1).wait_recv()
+
+        second_coef(jnp.maximum(i - 1, 0), lax.rem(i + 1, 2))
 
         def send():
             @pl.when(i == 0)
             def _():
-                first_copy(LEAVES - 1).start()
+                first_copy(last).start()
 
             @pl.when(i >= 1)
             def _():
@@ -361,9 +403,7 @@
             def _():
                 pair_copy(i - 2).start()
 
-        product(1, i, *units[0])
         leaf_pass(1, i, {1: pair, 2: send, 3: send_pair})
-        second_send[i] = contract(row_two, i)
         return carry
 
     def add_pair(i):
@@ -371,9 +411,14 @@
         pair_send[i] = (second_send[i] + second_recv[i]).astype(jnp.bfloat16)
 
     lax.fori_loop(0, LEAVES, pass_b, 0)
+    second_coef(last, last % 2)
+    pair_copy(0).wait_recv()
+    product(2, 0, *units[0])
 
     def pass_c(i, carry):
-        pair_copy(i).wait_recv()
+        @pl.when(i < last)
+        def _():
+            pair_copy(i + 1).wait_recv()
 
         @pl.when(i >= 2)
         def _():
@@ -383,7 +428,7 @@
         def send():
             @pl.when(i == 0)
             def _():
-                second_copy(LEAVES - 1).start()
+                second_copy(last).start()
 
         def pair():
             @pl.when(i < 2)
@@ -395,7 +440,6 @@
             def _():
                 pair_copy(i + LEAVES - 2).start()
 
-        product(2, i, *units[0])
         leaf_pass(2, i, {1: pair, 2: send, 3: send_pair})
         out_copy(i, 0).start()
         out_copy(i, 1).start()
@@ -462,8 +506,10 @@
     peaks = stats[:, :, 0:1]
     top = jnp.max(peaks, axis=0)
     whole = jnp.sum(stats[:, :, 1:2] * jnp.exp(peaks - top[None]), axis=0)
-    mean_out[...] = (top + jnp.log(whole / TOTAL)) / M
-    sample_out[...] = jnp.sum(sums_all[...], axis=0) / (LEAVES * n_leaf * M)
+    mean = (top + jnp.log(whole / TOTAL)) / M
+    mean_out[...] = jnp.broadcast_to(mean, (LEAVES, SUB)).T[0:1]
+    total = jnp.sum(sums_all[...], axis=0) / (LEAVES * n_leaf * M)
+    sample_out[...] = total.reshape(COLS)
 
 
 def per_device(limits, inv_scale, lower_blocks, qmc_gen, col_one, row_one, col_two, row_two):
@@ -472,23 +518,26 @@
     f32, bf16 = jnp.float32, jnp.bfloat16
     n_leaf, n_samp = lax.axis_size("leaf"), lax.axis_size("samp")
     dma = pltpu.SemaphoreType.DMA
+    bases = [jnp.swapaxes(v, 2, 3) for v in (col_one, row_one, col_two, row_two)]
     draws, mean_log, sample_log = pl.pallas_call(
         kernel,
         out_shape=(
             jax.ShapeDtypeStruct((LEAVES, 1, M, COLS), bf16),
-            jax.ShapeDtypeStruct((LEAVES, 1), f32),
-            jax.ShapeDtypeStruct((1, COLS), f32),
+            jax.ShapeDtypeStruct((1, LEAVES), f32),
+            jax.ShapeDtypeStruct((COLS,), f32),
         ),
         in_specs=[vmem, vmem, anywhere, vmem, anywhere, anywhere, anywhere, anywhere],
         out_specs=(anywhere, vmem, vmem),
         scratch_shapes=[
             pltpu.VMEM((LEAVES, M, M), bf16),
-            pltpu.VMEM((LEAVES, M, R), bf16),
-            pltpu.VMEM((LEAVES, M, R), bf16),
-            pltpu.VMEM((LEAVES, M, R), bf16),
-            pltpu.VMEM((LEAVES, M, R), bf16),
+            pltpu.VMEM((LEAVES, 2 * R, M), bf16),
+            pltpu.VMEM((LEAVES, R, M), bf16),
+            pltpu.VMEM((LEAVES, R, M), bf16),
+            pltpu.VMEM((LEAVES, M, 2 * R), bf16),
+            pltpu.VMEM((LEAVES, M, 2 * R), bf16),
+            pltpu.VMEM((LEAVES, M, SUB), bf16),
+            pltpu.VMEM((9, 8, 128), f32),
             pltpu.VMEM((LEAVES, M, COLS), f32),
-            pltpu.VMEM((LEAVES, M, SUB), f32),
             pltpu.VMEM((LEAVES, M, SUB), f32),
             pltpu.VMEM((SUB, HALF), f32),
             pltpu.VMEM((SUB, HALF), f32),
@@ -516,8 +565,8 @@
             collective_id=0, has_side_effects=True, vmem_limit_bytes=60 * 1024 * 1024
         ),
         name="conditioning",
-    )(limits, inv_scale, lower_blocks, qmc_gen, col_one, row_one, col_two, row_two)
-    return draws, mean_log, sample_log[0]
+    )(limits, inv_scale, lower_blocks, qmc_gen, *bases)
+    return draws, mean_log.T, sample_log
 
 
 def solution(mesh):

time: 106 us -> 88.4 us (0.83)
  local copies, waits for them, and re-layouts: 14.8 us -> 5.57 us
  Pallas kernels: 90.4 us -> 81.9 us
    unnamed x11 -> x7, local copies, waits for them, and re-layouts: 14.8 us -> 5.57 us
    pallas_call x1, Pallas kernels: 90.4 us -> 81.9 us  [per_device(): pl.pallas_call(kernel, out_shape=(jax.ShapeDtypeStruct((LEAVES, 1, M, COL...]
where the time goes in v2:
time: 88.4 us; the launch traced here: 88.1 us
  Pallas kernels  81.9 us (93%)
  local copies, waits for them, and re-layouts  5.57 us (6%)
    pallas_call x1, Pallas kernels, per_device(): pl.pallas_call(kernel, out_shape=(jax.ShapeDtypeStruct((LEAVES, 1, M, COL...  81.9 us
    unnamed x7, local copies, waits for them, and re-layouts  5.57 us

profile of v2, /device:TPU:2, one launch (start us, length us, event | category | flops | bytes accessed | tf_op | source)
XLA Modules:
  0.0 88.1 jit_solution(15784707339355579016)
XLA Ops:
  0.6 81.9 %conditioning.1 = (bf16[8,1,512,512]{3,2,1,0:T(8,128)(2,1)}, f32[1,8]{1,0:T(1,128)}, f32[512]{0:T(512)}) custom-call(f32[8,1,512]{2,1,0:T(1,128)} %limits.1, f32[8,1,512]{2,1,0:T(1,128)} %scales.1, bf16[8,1,512,512]{3,2,1,0:T(8,128)(2,1)} %lower_hbm.1, s32[8,1,512]{2,1,0:T(1,128)} %gens.1, bf16[8,1,64,512]{3,2,1,0:T(8,128)(2,1)} %bitcast.5, ...), custom_call_target="tpu_custom_call" | custom-call | tf_op jit(solution)/shard_map/conditioning/pallas_call | solution.py:522
  82.6 0.0 copy-start.1
  82.6 0.0 copy-start
  82.6 4.5 %copy.14 = bf16[8,1,512,512]{3,2,1,0:T(8,128)(2,1)} copy(bf16[8,1,512,512]{3,2,1,0:T(8,128)(2,1)} %get-tuple-element.12) | data formatting | bytes 8388608
  87.0 0.0 copy-done.1
  87.1 0.5 copy.15
  87.6 0.0 copy-done
  87.6 0.6 copy.16
Async XLA Ops:
  82.6 4.5 %copy-start.1 = (f32[1,8]{1,0:T(1,128)S(1)}, f32[1,8]{1,0:T(1,128)}, u32[]{:S(2)}) copy-start(f32[1,8]{1,0:T(1,128)} %get-tuple-element.7) | copy-start | bytes 100
  82.6 5.0 %copy-start = (f32[512]{0:T(512)S(1)}, f32[512]{0:T(512)}, u32[]{:S(2)}) copy-start(f32[512]{0:T(512)} %get-tuple-element.14) | copy-start | bytes 6148

commit v3 on v2

--- a/solution.py
+++ b/solution.py
@@ -73,8 +73,8 @@
     return jnp.where(z < ERFC_FROM, lax.exp2(tail), lax.erf(z) + 1.0)
 
 
-def quantile(p, centre_coefs):
-    mono = [tile(c, p.shape) for c in centre_coefs]
+def quantile(p):
+    mono = mono_a[1:] + mono_b[2:]
     centre = p - 0.5 * K
     square = centre * centre
     small = jnp.minimum(p, K - p)
@@ -90,11 +90,6 @@
         low = low * var + jnp.where(tail, d, b)
     scale = jnp.clip(centre, -EDGE, EDGE)
     return scale * top / low
-
-
-def tile(block, shape):
-    block = jnp.concatenate([block] * (shape[1] // 128), axis=1)
-    return jnp.concatenate([block] * (shape[0] // 8), axis=0)
 
 
 def kernel(
@@ -116,7 +111,6 @@
     cols_b,
     cols_c,
     tops,
-    table,
     points,
     scale_b,
     acc_0,
@@ -168,17 +162,12 @@
             dst = dst.at[R:]
         return pltpu.make_async_copy(src.at[i, 0], dst, load_sem.at[which, i])
 
-    def start_loads(which):
-        def body(i, carry):
+    def start_loads(i, carry):
+        for which in (3, 4, 0, 1, 2):
             load(which, i).start()
-            return carry
-
-        lax.fori_loop(0, LEAVES, body, 0)
-
-    for which in (0, 3, 4, 1, 2):
-        start_loads(which)
-    for at, value in enumerate(mono_a[1:] + mono_b[2:]):
-        table[at] = jnp.full((8, 128), value, jnp.float32)
+        return carry
+
+    lax.fori_loop(0, LEAVES, start_loads, 0)
     for h in range(2):
         draw[h][1] = jnp.zeros((M, HALF), jnp.bfloat16)
     row = lax.broadcasted_iota(jnp.int32, (SUB, HALF), 0)
@@ -289,8 +278,7 @@
                 points[i, rows, cols] = u
             else:
                 u = points[i, rows, cols]
-            coefs = [table[j] for j in range(9)]
-            draw[h][par, rows, :] = quantile(u * y, coefs).astype(jnp.bfloat16)
+            draw[h][par, rows, :] = quantile(u * y).astype(jnp.bfloat16)
             if step == 2:
                 group.append(y[:8] * y[8:])
                 if len(group) == 2:
@@ -305,11 +293,9 @@
 
     units = [(s, h) for s in range(M // SUB) for h in range(2)]
 
-    def leaf_pass(step, i, hooks, limit_0=None):
+    def leaf_pass(step, i, limit_0=None):
         gen_b = None
         for at, (s, h) in enumerate(units):
-            if at in hooks:
-                hooks[at]()
             if at + 1 < len(units):
                 if step > 0 or units[at + 1][0] > 0:
                     product(step, i, *units[at + 1])
@@ -335,6 +321,15 @@
     def pass_a(i, carry):
         for which in (0, 1, 3, 4):
             load(which, i).wait()
+
+        @pl.when(i == 2)
+        def _():
+            pl.semaphore_wait(barrier, n_leaf + n_samp - 2)
+
+        @pl.when(i >= 2)
+        def _():
+            first_copy(i - 2).start()
+
         before = jnp.maximum(i - 1, 0)
         first_coef(before, lax.rem(i + 1, 2))
         limit = -limits[i]
@@ -358,19 +353,11 @@
             cols_c[i, rows, :] = pair.T
             cols_b[i, rows, :] = jnp.concatenate([pair[:R], part[:R]], axis=0).T
 
-        def send():
-            @pl.when(i == 1)
-            def _():
-                pl.semaphore_wait(barrier, n_leaf + n_samp - 2)
-
-            @pl.when(i >= 1)
-            def _():
-                first_copy(i - 1).start()
-
-        leaf_pass(0, i, {2: send}, limit_0)
+        leaf_pass(0, i, limit_0)
         return carry
 
     lax.fori_loop(0, LEAVES, pass_a, 0)
+    first_copy(last - 1).start()
     first_coef(last, last % 2)
     first_copy(0).wait_recv()
     product(1, 0, *units[0])
@@ -382,28 +369,24 @@
         def _():
             first_copy(i + 1).wait_recv()
 
+        @pl.when(i == 0)
+        def _():
+            first_copy(last).start()
+
+        @pl.when(i >= 2)
+        def _():
+            second_copy(i - 2).start()
+
+        @pl.when(i >= 4)
+        def _():
+            pair_copy(i - 4).start()
+
+        @pl.when(i >= 3)
+        def _():
+            add_pair(i - 3)
+
         second_coef(jnp.maximum(i - 1, 0), lax.rem(i + 1, 2))
-
-        def send():
-            @pl.when(i == 0)
-            def _():
-                first_copy(last).start()
-
-            @pl.when(i >= 1)
-            def _():
-                second_copy(i - 1).start()
-
-        def pair():
-            @pl.when(i >= 2)
-            def _():
-                add_pair(i - 2)
-
-        def send_pair():
-            @pl.when(i >= 2)
-            def _():
-                pair_copy(i - 2).start()
-
-        leaf_pass(1, i, {1: pair, 2: send, 3: send_pair})
+        leaf_pass(1, i)
         return carry
 
     def add_pair(i):
@@ -425,22 +408,19 @@
             out_copy(i - 2, 0).wait()
             out_copy(i - 2, 1).wait()
 
-        def send():
-            @pl.when(i == 0)
-            def _():
-                second_copy(last).start()
-
-        def pair():
-            @pl.when(i < 2)
-            def _():
-                add_pair(i + LEAVES - 2)
-
-        def send_pair():
-            @pl.when(i < 2)
-            def _():
-                pair_copy(i + LEAVES - 2).start()
-
-        leaf_pass(2, i, {1: pair, 2: send, 3: send_pair})
+        @pl.when(i < 2)
+        def _():
+            second_copy(i + LEAVES - 2).start()
+
+        @pl.when(i < 4)
+        def _():
+            pair_copy(i + LEAVES - 4).start()
+
+        @pl.when(i < 3)
+        def _():
+            add_pair(i + LEAVES - 3)
+
+        leaf_pass(2, i)
         out_copy(i, 0).start()
         out_copy(i, 1).start()
         return carry
@@ -536,7 +516,6 @@
             pltpu.VMEM((LEAVES, M, 2 * R), bf16),
             pltpu.VMEM((LEAVES, M, 2 * R), bf16),
             pltpu.VMEM((LEAVES, M, SUB), bf16),
-            pltpu.VMEM((9, 8, 128), f32),
             pltpu.VMEM((LEAVES, M, COLS), f32),
             pltpu.VMEM((LEAVES, M, SUB), f32),
             pltpu.VMEM((SUB, HALF), f32),

time: 88.4 us -> 84.4 us (0.955)
  Pallas kernels: 81.9 us -> 77.9 us
    pallas_call x1, Pallas kernels: 81.9 us -> 77.9 us  [per_device(): pl.pallas_call(kernel, out_shape=(jax.ShapeDtypeStruct((LEAVES, 1, M, COL...]
where the time goes in v3:
time: 84.4 us; the launch traced here: 84.1 us
  Pallas kernels  77.9 us (92%)
  local copies, waits for them, and re-layouts  5.57 us (7%)
    pallas_call x1, Pallas kernels, per_device(): pl.pallas_call(kernel, out_shape=(jax.ShapeDtypeStruct((LEAVES, 1, M, COL...  77.9 us
    unnamed x7, local copies, waits for them, and re-layouts  5.57 us

profile of v3, /device:TPU:2, one launch (start us, length us, event | category | flops | bytes accessed | tf_op | source)
XLA Modules:
  0.0 84.1 jit_solution(16563163646829592128)
XLA Ops:
  0.6 77.9 %conditioning.1 = (bf16[8,1,512,512]{3,2,1,0:T(8,128)(2,1)}, f32[1,8]{1,0:T(1,128)}, f32[512]{0:T(512)}) custom-call(f32[8,1,512]{2,1,0:T(1,128)} %limits.1, f32[8,1,512]{2,1,0:T(1,128)} %scales.1, bf16[8,1,512,512]{3,2,1,0:T(8,128)(2,1)} %lower_hbm.1, s32[8,1,512]{2,1,0:T(1,128)} %gens.1, bf16[8,1,64,512]{3,2,1,0:T(8,128)(2,1)} %bitcast.5, ...), custom_call_target="tpu_custom_call" | custom-call | tf_op jit(solution)/shard_map/conditioning/pallas_call | solution.py:502
  78.5 0.0 copy-start.1
  78.6 0.0 copy-start
  78.6 4.5 %copy.14 = bf16[8,1,512,512]{3,2,1,0:T(8,128)(2,1)} copy(bf16[8,1,512,512]{3,2,1,0:T(8,128)(2,1)} %get-tuple-element.12) | data formatting | bytes 8388608
  83.0 0.0 copy-done.1
  83.0 0.5 copy.15
  83.6 0.0 copy-done
  83.6 0.6 copy.16
Async XLA Ops:
  78.5 4.5 %copy-start.1 = (f32[1,8]{1,0:T(1,128)S(1)}, f32[1,8]{1,0:T(1,128)}, u32[]{:S(2)}) copy-start(f32[1,8]{1,0:T(1,128)} %get-tuple-element.7) | copy-start | bytes 100
  78.6 5.0 %copy-start = (f32[512]{0:T(512)S(1)}, f32[512]{0:T(512)}, u32[]{:S(2)}) copy-start(f32[512]{0:T(512)} %get-tuple-element.14) | copy-start | bytes 6148

commit v4 on v3

--- a/solution.py
+++ b/solution.py
@@ -54,6 +54,34 @@
 mono_c = tuple(v / coef_c[0] * G**-j for j, v in enumerate(coef_c))
 mono_d = tuple(EDGE / TAIL * v / coef_d[0] * G**-j for j, v in enumerate(coef_d))
 
+
+def fewer_products(mono):
+    def shifted(by):
+        out = list(mono)
+        for stop in range(len(out), 1, -1):
+            for j in range(1, stop):
+                out[j] -= by * out[j - 1]
+        return out
+
+    def gap(by):
+        q = shifted(by)
+        return q[3] - q[1] * q[2]
+
+    low, high = -64.0, 64.0
+    rising = gap(high) > gap(low)
+    for _ in range(200):
+        middle = 0.5 * (low + high)
+        if (gap(middle) > 0.0) == rising:
+            high = middle
+        else:
+            low = middle
+    q = shifted(low)
+    return (low, q[2], q[4], q[1] + low, q[5] - q[4] * q[1])
+
+
+top_a = fewer_products(mono_a)
+top_c = fewer_products(mono_c)
+
 ROOT_HALF = math.sqrt(0.5)
 FLOOR = -6.0 * ROOT_HALF
 ERFC_FROM = -3.5 * ROOT_HALF
@@ -73,8 +101,7 @@
     return jnp.where(z < ERFC_FROM, lax.exp2(tail), lax.erf(z) + 1.0)
 
 
-def quantile(p):
-    mono = mono_a[1:] + mono_b[2:]
+def quantile(p, held):
     centre = p - 0.5 * K
     square = centre * centre
     small = jnp.minimum(p, K - p)
@@ -82,21 +109,22 @@
     depth = math.log2(K) - jnp.log2(small)
     depth = depth * lax.rsqrt(depth)
     var = jnp.where(tail, depth, square)
-    top = var + jnp.where(tail, mono_c[1], mono[0])
-    for c, a in zip(mono_c[2:], mono[1:5]):
-        top = top * var + jnp.where(tail, c, a)
+    e = [jnp.where(tail, c, a) for c, a in zip(top_c, (held[0], held[1], held[2], held[3], held[4]))]
+    y = var + e[0]
+    y = y * y
+    top = ((y + e[1]) * y + e[2]) * (var + e[3]) + e[4]
     low = jnp.where(tail, mono_d[0], square + mono_b[1])
-    for d, b in zip(mono_d[1:], mono[5:]):
+    for d, b in zip(mono_d[1:], (mono_b[2], mono_b[3], mono_b[4], mono_b[5])):
         low = low * var + jnp.where(tail, d, b)
     scale = jnp.clip(centre, -EDGE, EDGE)
     return scale * top / low
 
 
 def kernel(
-    limits,
-    scales,
+    limits_hbm,
+    scales_hbm,
     lower_hbm,
-    gens,
+    gens_hbm,
     col_one_hbm,
     row_one_hbm,
     col_two_hbm,
@@ -104,6 +132,9 @@
     draws_hbm,
     mean_out,
     sample_out,
+    limits,
+    scales,
+    gens,
     lower,
     cols_t,
     row_one,
@@ -111,8 +142,10 @@
     cols_b,
     cols_c,
     tops,
+    table,
     points,
     scale_b,
+    cdf_0,
     acc_0,
     acc_1,
     draw_0,
@@ -127,6 +160,7 @@
     pair_recv,
     stat_all,
     sums_all,
+    row_sem,
     load_sem,
     out_sem,
     first_sems,
@@ -167,7 +201,17 @@
             load(which, i).start()
         return carry
 
+    row_loads = [
+        pltpu.make_async_copy(src, dst, row_sem.at[at])
+        for at, (src, dst) in enumerate(
+            ((limits_hbm, limits), (scales_hbm, scales), (gens_hbm, gens))
+        )
+    ]
+    for copy in row_loads:
+        copy.start()
     lax.fori_loop(0, LEAVES, start_loads, 0)
+    for at, value in enumerate((top_a[0], top_a[1], top_a[2], top_a[3], top_a[4],)):
+        table[at] = jnp.full((CHUNK, HALF), value, jnp.float32)
     for h in range(2):
         draw[h][1] = jnp.zeros((M, HALF), jnp.bfloat16)
     row = lax.broadcasted_iota(jnp.int32, (SUB, HALF), 0)
@@ -261,7 +305,11 @@
             here = slice(chunk * CHUNK, (chunk + 1) * CHUNK)
             scale = scale_b[i, rows, :]
             if step == 0 and s == 0:
-                y = twice_cdf(jnp.maximum(scale * limit_0[here, :], FLOOR))
+                if h == 0:
+                    y = twice_cdf(jnp.maximum(scale * limit_0[here, :], FLOOR))
+                    cdf_0[here, :] = y
+                else:
+                    y = cdf_0[here, :]
                 y = jnp.concatenate([y, y], axis=1)
             else:
                 scale = jnp.concatenate([scale, scale], axis=1)
@@ -278,7 +326,7 @@
                 points[i, rows, cols] = u
             else:
                 u = points[i, rows, cols]
-            draw[h][par, rows, :] = quantile(u * y).astype(jnp.bfloat16)
+            draw[h][par, rows, :] = quantile(u * y, [table[j] for j in range(5)]).astype(jnp.bfloat16)
             if step == 2:
                 group.append(y[:8] * y[8:])
                 if len(group) == 2:
@@ -356,6 +404,8 @@
         leaf_pass(0, i, limit_0)
         return carry
 
+    for copy in row_loads:
+        copy.wait()
     lax.fori_loop(0, LEAVES, pass_a, 0)
     first_copy(last - 1).start()
     first_coef(last, last % 2)
@@ -498,6 +548,7 @@
     f32, bf16 = jnp.float32, jnp.bfloat16
     n_leaf, n_samp = lax.axis_size("leaf"), lax.axis_size("samp")
     dma = pltpu.SemaphoreType.DMA
+    stay = functools.partial(pltpu.with_memory_space_constraint, memory_space=pltpu.HBM)
     bases = [jnp.swapaxes(v, 2, 3) for v in (col_one, row_one, col_two, row_two)]
     draws, mean_log, sample_log = pl.pallas_call(
         kernel,
@@ -506,9 +557,12 @@
             jax.ShapeDtypeStruct((1, LEAVES), f32),
             jax.ShapeDtypeStruct((COLS,), f32),
         ),
-        in_specs=[vmem, vmem, anywhere, vmem, anywhere, anywhere, anywhere, anywhere],
+        in_specs=[anywhere] * 8,
         out_specs=(anywhere, vmem, vmem),
         scratch_shapes=[
+            pltpu.VMEM((LEAVES, 1, M), f32),
+            pltpu.VMEM((LEAVES, 1, M), f32),
+            pltpu.VMEM((LEAVES, 1, M), jnp.int32),
             pltpu.VMEM((LEAVES, M, M), bf16),
             pltpu.VMEM((LEAVES, 2 * R, M), bf16),
             pltpu.VMEM((LEAVES, R, M), bf16),
@@ -516,8 +570,10 @@
             pltpu.VMEM((LEAVES, M, 2 * R), bf16),
             pltpu.VMEM((LEAVES, M, 2 * R), bf16),
             pltpu.VMEM((LEAVES, M, SUB), bf16),
+            pltpu.VMEM((5, CHUNK, HALF), f32),
             pltpu.VMEM((LEAVES, M, COLS), f32),
             pltpu.VMEM((LEAVES, M, SUB), f32),
+            pltpu.VMEM((SUB, SUB), f32),
             pltpu.VMEM((SUB, HALF), f32),
             pltpu.VMEM((SUB, HALF), f32),
             pltpu.VMEM((2, M, HALF), bf16),
@@ -532,6 +588,7 @@
             pltpu.VMEM((LEAVES, R, COLS), bf16),
             pltpu.VMEM((n_samp, LEAVES, SUB), f32),
             pltpu.VMEM((n_leaf, 1, COLS), f32),
+            dma((3,)),
             dma((5, LEAVES)),
             dma((2, LEAVES)),
             dma((2, LEAVES)),
@@ -541,10 +598,10 @@
             dma((2, n_leaf)),
         ],
         compiler_params=pltpu.CompilerParams(
-            collective_id=0, has_side_effects=True, vmem_limit_bytes=60 * 1024 * 1024
+            collective_id=0, has_side_effects=True, vmem_limit_bytes=40 * 1024 * 1024
         ),
         name="conditioning",
-    )(limits, inv_scale, lower_blocks, qmc_gen, *bases)
+    )(*map(stay, (limits, inv_scale, lower_blocks, qmc_gen, *bases)))
     return draws, mean_log.T, sample_log
 
 

time: 84.4 us -> 80.3 us (0.951)
  local copies, waits for them, and re-layouts: 5.57 us -> 3.1 us
  Pallas kernels: 77.9 us -> 76.3 us
    unnamed x7 -> x3, local copies, waits for them, and re-layouts: 5.57 us -> 3.1 us
    pallas_call x1, Pallas kernels: 77.9 us -> 76.3 us  [per_device(): pl.pallas_call(kernel, out_shape=(jax.ShapeDtypeStruct((LEAVES, 1, M, COL...]
where the time goes in v4:
time: 80.3 us; the launch traced here: 80.1 us
  Pallas kernels  76.3 us (95%)
  local copies, waits for them, and re-layouts  3.1 us (4%)
    pallas_call x1, Pallas kernels, per_device(): pl.pallas_call(kernel, out_shape=(jax.ShapeDtypeStruct((LEAVES, 1, M, COL...  76.3 us
    unnamed x3, local copies, waits for them, and re-layouts  3.1 us

profile of v4, /device:TPU:2, one launch (start us, length us, event | category | flops | bytes accessed | tf_op | source)
XLA Modules:
  0.0 80.1 jit_solution(7050164804104743762)
XLA Ops:
  0.6 76.3 %conditioning.1 = (bf16[8,1,512,512]{3,2,1,0:T(8,128)(2,1)S(1)}, f32[1,8]{1,0:T(1,128)S(1)}, f32[512]{0:T(512)S(1)}) custom-call(f32[8,1,512]{2,1,0:T(1,128)} %limits_hbm.1, f32[8,1,512]{2,1,0:T(1,128)} %scales_hbm.1, bf16[8,1,512,512]{3,2,1,0:T(8,128)(2,1)} %lower_hbm.1, s32[8,1,512]{2,1,0:T(1,128)} %gens_hbm.1, bf16[8,1,64,512]{3,2,1,0:T(8,128)(2,1)} %bitcast.6, ...), custom_call_target="tpu_custom_call" | custom-call | tf_op jit(solution)/shard_map/conditioning/pallas_call | solution.py:553
  77.0 2.0 %copy.14 = bf16[8,1,512,512]{3,2,1,0:T(8,128)(2,1)} copy(bf16[8,1,512,512]{3,2,1,0:T(8,128)(2,1)S(1)} %get-tuple-element.12) | data formatting | bytes 8388608
  79.0 0.5 copy.15
  79.5 0.6 copy.16
